TPU v7x, 512 devices: a whole 4x8x8 slice. The times are simulated.
512 devices in a mesh: lat: 128 (over z, y, core), tok: 4 (over x).
Axes of the slice: x: 4, y: 8, z: 8, core: 2. Of those that a mesh axis runs over, the one named last changes fastest.
Arguments:
- resid_stream: bfloat16 [384, 8192], P('lat', 'tok'), may hold values from -6 to 6
- enc_weight: bfloat16 [16384, 8192], P('lat', 'tok'), may hold values from -0.0625 to 0.0625
- enc_bias: float32 [16384], P('lat'), may hold values from -3 to 3
- dec_weight: bfloat16 [16384, 8192], P('lat', 'tok'), may hold values from -0.75 to 0.75
- dec_bias: float32 [8192], P('tok'), may hold values from -3 to 3
- active_ids: int32 [384, 64], replicated, may hold values from 0 to 16383, as said below
- active_count: int32 [384], replicated, may hold values from 32 to 64, as said below
Outputs:
- pre_acts: float32 [384, 16384], P(None, 'lat')
- residual: bfloat16 [384, 8192], P('lat', 'tok')
- grad_enc: bfloat16 [16384, 8192], P('lat', 'tok')
- grad_dec: bfloat16 [16384, 8192], P('lat', 'tok')
Inputs may be any that keep to these rules, and one draw needn't show every extreme that they name: `active_ids`: within a row all 64 entries are different latents; entries past the row's count are ordinary latent numbers that are to be ignored; some latent shards are named far more often than others. `active_count`: some row has 64 valid entries and some has 32.
All inputs are finite; a program needn't handle non-finite values.
Results may differ from a plain program's by a relative error of at most 0.0059.
Values may be sent and summed in bfloat16 or wider, within the bound.
A program may use at most 64 MiB of HBM per device.

v0:
```python
import math
import jax
import jax.numpy as jnp
from jax import lax
from jax.sharding import PartitionSpec as P


def active_mask(id_rows, counts, first_latent, latent_count):
    tokens, top_count = id_rows.shape
    block_rows = math.gcd(tokens, 128)
    in_list = jnp.arange(top_count, dtype=jnp.int32)[None, :] < counts[:, None]
    local_ids = jnp.where(in_list, id_rows - first_latent, -1)
    latent_iota = jnp.arange(latent_count, dtype=jnp.int32)

    def one_block(id_block):
        return jnp.any(id_block[:, :, None] == latent_iota[None, None, :], axis=1).astype(
            jnp.float32
        )

    blocks = lax.map(one_block, local_ids.reshape(tokens // block_rows, block_rows, top_count))
    return blocks.reshape(tokens, latent_count)


def shards(resid_stream, enc_weight, enc_bias, dec_weight, dec_bias, active_ids, active_count):
    lat_dev = enc_weight.shape[0]
    rows_own = resid_stream.shape[0]
    full_rows = lax.all_gather(resid_stream, "lat", axis=0, tiled=True)
    partial_value = lax.dot_general(
        full_rows, enc_weight, (((1,), (1,)), ((), ())), preferred_element_type=jnp.float32
    )
    pre_acts = lax.psum(partial_value, "tok") + enc_bias[None, :]
    act_mask = active_mask(active_ids, active_count, lax.axis_index("lat") * lat_dev, lat_dev)
    activations = (pre_acts * act_mask).astype(jnp.bfloat16)
    own_start = lax.axis_index("lat") * rows_own
    rebuilt = lax.psum(jnp.dot(activations, dec_weight, preferred_element_type=jnp.float32), "lat")
    residual_all = (rebuilt + dec_bias[None, :] - full_rows.astype(jnp.float32)).astype(
        jnp.bfloat16
    )
    residual = lax.dynamic_slice_in_dim(residual_all, own_start, rows_own, 0)
    grad_dec = 0.5 * lax.dot_general(
        activations, residual_all, (((0,), (0,)), ((), ())), preferred_element_type=jnp.float32
    )
    back_terms = lax.dot_general(
        residual_all, dec_weight, (((1,), (1,)), ((), ())), preferred_element_type=jnp.float32
    )
    back_terms = lax.psum(back_terms, "tok")
    act_grads = (0.5 * back_terms * act_mask).astype(jnp.bfloat16)
    grad_enc = lax.dot_general(
        act_grads, full_rows, (((0,), (0,)), ((), ())), preferred_element_type=jnp.float32
    )
    return (pre_acts, residual, grad_enc.astype(jnp.bfloat16), grad_dec.astype(jnp.bfloat16))


def solution(mesh):
    placed = (P("lat", "tok"), P("lat", "tok"), P("lat"), P("lat", "tok"), P("tok"), P(), P())
    return jax.shard_map(
        shards,
        mesh=mesh,
        in_specs=placed,
        out_specs=(P(None, "lat"), P("lat", "tok"), P("lat", "tok"), P("lat", "tok")),
        check_vma=False,
    )
```

profile of v0, /device:TPU:8, one launch (start us, length us, event | category | flops | bytes accessed | tf_op | source)
XLA Modules:
  0.0 428.0 jit_solution(15382301777076680504)
XLA Ops:
  7.2 0.0 copy-start
  7.2 0.0 all-gather.3.cloned.1.call-start
  7.2 0.7 all-gather.3.cloned.1.call-update
  7.9 0.0 all-reduce.4.cloned.1.call-start
  8.0 0.9 subtract_select_fusion
  8.9 0.1 copy.14
  9.0 0.0 copy-start.2
  9.0 89.1 %all-gather.3.cloned.1.call-done = bf16[128,3,2048]{2,1,0:T(4,128)(2,1)} async-done(((bf16[1,3,2048]{2,1,0:T(4,128)(2,1)}), bf16[128,3,2048]{2,1,0:T(4,128)(2,1)}) %all-gather.3.cloned.1.call-update) | async-done | bytes 1572880 | tf_op jit(solution)/shard_map/all_gather | solution.py:27
  98.2 3.9 reshape.33
  102.1 0.0 copy-done.2
  102.1 0.0 copy-start.4
  102.1 1.3 fusion.6
  103.4 0.0 all-reduce.4.cloned.1.call-update
  103.4 0.0 all-reduce.6.cloned.1.call-start
  103.4 4.4 %while.11 = (s32[]{:T(128)}, f32[3,128,128]{2,1,0:T(8,128)S(1)}, s32[3,128,64]{2,1,0:T(8,128)S(1)}, s32[]{:T(128)}) while((s32[]{:T(128)}, f32[3,128,128]{2,1,0:T(8,128)S(1)}, s32[3,128,64]{2,1,0:T(8,128)S(1)}, s32[]{:T(128)}) %tuple.37), condition=%wide.region_3.4_spmd.clone, body=%wide.region_1.3_spmd.clone.sunk | while | flops 2097154 | bytes 196677 | solution.py:20
  103.5 1.4 fusion.20
  104.9 1.4 fusion.20
  106.4 1.4 fusion.20
  107.8 45.5 %all-reduce.4.cloned.1.call-done = f32[384,128]{1,0:T(8,128)} async-done(((f32[384,128]{1,0:T(8,128)}), f32[384,128]{1,0:T(8,128)}) %all-reduce.4.cloned.1.call-update) | async-done | bytes 196624 | tf_op jit(solution)/shard_map/psum | solution.py:31
  153.4 0.0 copy-done.4
  153.4 1.6 fusion.4
  155.0 0.0 copy-done
  155.0 2.2 fusion.7
  157.2 0.0 copy-start.3
  157.2 0.0 all-reduce.6.cloned.1.call-update
  157.3 0.0 all-reduce.8.cloned.1.call-start
  157.3 204.0 %all-reduce.6.cloned.1.call-done = f32[384,2048]{1,0:T(8,128)} async-done(((f32[384,2048]{1,0:T(8,128)}), f32[384,2048]{1,0:T(8,128)}) %all-reduce.6.cloned.1.call-update) | async-done | bytes 3145744 | tf_op jit(solution)/shard_map/psum | solution.py:35
  361.3 0.0 copy-done.3
  361.3 2.4 subtract_convert_fusion
  363.8 0.0 copy-start.1
  363.8 1.1 copy-done.1
  364.9 1.3 fusion.8
  366.2 2.7 fusion.3
  368.9 0.0 all-reduce.8.cloned.1.call-update
  368.9 1.5 constant_dynamic-slice_fusion
  370.4 48.8 %all-reduce.8.cloned.1.call-done = f32[384,128]{1,0:T(8,128)} async-done(((f32[384,128]{1,0:T(8,128)}), f32[384,128]{1,0:T(8,128)}) %all-reduce.8.cloned.1.call-update) | async-done | bytes 196624 | tf_op jit(solution)/shard_map/psum | solution.py:46
  419.2 1.0 fusion.5
  420.2 1.3 convolution_convert_fusion
  (7 shorter events, 0.1 us)
Async XLA Ops:
  7.2 147.8 %copy-start = (bf16[128,2048]{1,0:T(8,128)(2,1)S(1)}, bf16[128,2048]{1,0:T(8,128)(2,1)}, u32[]{:S(2)}) copy-start(bf16[128,2048]{1,0:T(8,128)(2,1)} %param.12) | copy-start | bytes 1572868
  7.2 91.0 %all-gather.3.cloned.1.call-start = ((), (), s32[]{:S(2)}) async-start(), calls=%async_computation.3 | async-start | bytes 2113536 | tf_op jit(solution)/shard_map/all_gather | solution.py:27
  7.9 145.4 %all-reduce.4.cloned.1.call-start = ((), (), s32[]{:S(2)}) async-start(), calls=%async_computation | async-start | bytes 393216 | tf_op jit(solution)/shard_map/psum | solution.py:31
  9.0 93.1 %copy-start.2 = (bf16[128,2048]{1,0:T(8,128)(2,1)S(1)}, bf16[128,2048]{1,0:T(8,128)(2,1)}, u32[]{:S(2)}) copy-start(bf16[128,2048]{1,0:T(8,128)(2,1)} %param.10) | copy-start | bytes 1572868
  102.1 51.3 %copy-start.4 = (f32[128]{0:T(128)S(1)}, f32[128]{0:T(128)}, u32[]{:S(2)}) copy-start(f32[128]{0:T(128)} %param.11) | copy-start | bytes 1540
  103.4 257.9 %all-reduce.6.cloned.1.call-start = ((), (), s32[]{:S(2)}) async-start(), calls=%async_computation.1 | async-start | bytes 6291456 | tf_op jit(solution)/shard_map/psum | solution.py:35
  157.2 204.1 %copy-start.3 = (f32[2048]{0:T(1024)S(1)}, f32[2048]{0:T(1024)}, u32[]{:S(2)}) copy-start(f32[2048]{0:T(1024)} %param.13) | copy-start | bytes 24580
  157.3 262.0 %all-reduce.8.cloned.1.call-start = ((), (), s32[]{:S(2)}) async-start(), calls=%async_computation.2 | async-start | bytes 393216 | tf_op jit(solution)/shard_map/psum | solution.py:46
  363.8 1.1 copy-start.1
Sparse Core Ops, SparseCore 0:
  11.1 87.0 all-gather.2
  103.5 49.7 all-reduce.3
  157.4 203.9 all-reduce.5
  369.0 50.1 all-reduce.7
where the time goes:
time: 428 us
  waiting for transfers between devices  388 us (91%)
  between operations  13.9 us (3%)
  other arithmetic  10.2 us (2%)
  matrix products  8.72 us (2%)
  local copies, waits for them, and re-layouts  6.7 us (2%)
    psum x1, waiting for transfers between devices, shards(): lax.psum(jnp.dot(activations, dec_weight, preferred_element_type=jnp.floa...  204 us
    all_gather x1, waiting for transfers between devices, shards(): full_rows = lax.all_gather(resid_stream, 'lat', axis=0, tiled=True)  89.1 us
    psum x1, waiting for transfers between devices, shards(): back_terms = lax.psum(back_terms, 'tok')  48.8 us
    psum x1, waiting for transfers between devices, shards(): pre_acts = lax.psum(partial_value, 'tok') + enc_bias[None, :]  45.5 us
  transfers between devices with their start and end apart: 4, of which 4 were waited for; matrix products, arithmetic and copies ran while one was open for 2% of the time, Pallas kernels for 0%

commit v1 on v0

--- a/solution.py
+++ b/solution.py
@@ -3,6 +3,13 @@
 import jax.numpy as jnp
 from jax import lax
 from jax.sharding import PartitionSpec as P
+from jax.lax import all_to_all, axis_size
+
+
+def wrap_bench(chunk, array_dim):
+    high = jnp.stack([chunk for _ in range(axis_size("lat"))], axis=0)
+    frame_out = all_to_all(high, "lat", 0, 0)
+    return jnp.concatenate(frame_out, array_dim)
 
 
 def active_mask(id_rows, counts, first_latent, latent_count):
@@ -24,7 +31,7 @@
 def shards(resid_stream, enc_weight, enc_bias, dec_weight, dec_bias, active_ids, active_count):
     lat_dev = enc_weight.shape[0]
     rows_own = resid_stream.shape[0]
-    full_rows = lax.all_gather(resid_stream, "lat", axis=0, tiled=True)
+    full_rows = wrap_bench(resid_stream, 0)
     partial_value = lax.dot_general(
         full_rows, enc_weight, (((1,), (1,)), ((), ())), preferred_element_type=jnp.float32
     )

time: 428 us -> 408 us (0.953)
  waiting for transfers between devices: 388 us -> 348 us
  starting transfers between devices: 0.16 us -> 18.1 us
    all_gather x1 -> x0, waiting for transfers between devices: 89.1 us -> none  [shards(): full_rows = lax.all_gather(resid_stream, 'lat', axis=0, tiled=True)]
    all_to_all x0 -> x1, waiting for transfers between devices: none -> 53.4 us  [wrap_bench(): frame_out = all_to_all(high, 'lat', 0, 0)]
    all_to_all x0 -> x1, starting transfers between devices: none -> 18 us  [wrap_bench(): frame_out = all_to_all(high, 'lat', 0, 0)]
  transfers between devices with their start and end apart: 4 -> 4, of which waited for: 4 -> 4; matrix products, arithmetic and copies ran while one was open for 2% -> 1% of each run, Pallas kernels for 0% -> 0%
where the time goes in v1:
time: 408 us; the launch traced here: 407 us
  waiting for transfers between devices  348 us (85%)
  starting transfers between devices  18.1 us (4%)
  between operations  13.9 us (3%)
  local copies, waits for them, and re-layouts  9.84 us (2%)
  other arithmetic  9.24 us (2%)
  matrix products  8.73 us (2%)
    psum x1, waiting for transfers between devices, shards(): lax.psum(jnp.dot(activations, dec_weight, preferred_element_type=jnp.floa...  204 us
    all_to_all x1, waiting for transfers between devices, wrap_bench(): frame_out = all_to_all(high, 'lat', 0, 0)  53.4 us
    psum x1, waiting for transfers between devices, shards(): back_terms = lax.psum(back_terms, 'tok')  48.9 us
    psum x1, waiting for transfers between devices, shards(): pre_acts = lax.psum(partial_value, 'tok') + enc_bias[None, :]  41.3 us
    all_to_all x1, starting transfers between devices, wrap_bench(): frame_out = all_to_all(high, 'lat', 0, 0)  18 us
  transfers between devices with their start and end apart: 4, of which 4 were waited for; matrix products, arithmetic and copies ran while one was open for 1% of the time, Pallas kernels for 0%

profile of v1, /device:TPU:8, one launch (start us, length us, event | category | flops | bytes accessed | tf_op | source)
XLA Modules:
  0.0 407.5 jit_solution(828840086550292007)
XLA Ops:
  7.2 0.0 copy-start
  7.2 3.1 stack.2
  10.3 0.0 copy-start.3
  10.3 0.0 copy-start.5
  10.3 18.0 %all-to-all-start = ((bf16[128,3,2048]{2,1,0:T(4,128)(2,1)}), bf16[128,3,2048]{2,1,0:T(4,128)(2,1)}, u32[]{:S(2)}, u32[]{:S(2)}) async-start(bf16[128,3,2048]{2,1,0:T(4,128)(2,1)} %stack.2), calls=%async_computation | async-start | bytes 4194304 | tf_op jit(solution)/shard_map/all_to_all | solution.py:11
  28.3 0.0 all-reduce.4.cloned.1.call-start
  28.3 0.0 copy-done.3
  28.4 0.0 copy-done.5
  28.4 0.1 copy.13
  28.5 0.0 copy-start.2
  28.5 53.4 %all-to-all-done = bf16[128,3,2048]{2,1,0:T(4,128)(2,1)} async-done(((bf16[128,3,2048]{2,1,0:T(4,128)(2,1)}), bf16[128,3,2048]{2,1,0:T(4,128)(2,1)}, u32[]{:S(2)}, u32[]{:S(2)}) %all-to-all-start) | async-done | bytes 1572896 | tf_op jit(solution)/shard_map/all_to_all | solution.py:11
  81.9 3.9 reshape.34
  85.9 0.0 copy-done.2
  85.9 0.0 copy-start.6
  85.9 1.3 fusion.6
  87.1 0.0 all-reduce.4.cloned.1.call-update
  87.2 0.0 all-reduce.6.cloned.1.call-start
  87.2 4.4 %while.11 = (s32[]{:T(128)}, f32[3,128,128]{2,1,0:T(8,128)S(1)}, s32[3,128,64]{2,1,0:T(8,128)S(1)}, s32[]{:T(128)}) while((s32[]{:T(128)}, f32[3,128,128]{2,1,0:T(8,128)S(1)}, s32[3,128,64]{2,1,0:T(8,128)S(1)}, s32[]{:T(128)}) %tuple.35), condition=%wide.region_3.4_spmd.clone, body=%wide.region_1.3_spmd.clone.sunk | while | flops 2097154 | bytes 196677 | solution.py:27
  87.2 1.4 fusion.20
  88.7 1.4 fusion.20
  90.2 1.4 fusion.20
  91.6 41.3 %all-reduce.4.cloned.1.call-done = f32[384,128]{1,0:T(8,128)} async-done(((f32[384,128]{1,0:T(8,128)}), f32[384,128]{1,0:T(8,128)}) %all-reduce.4.cloned.1.call-update) | async-done | bytes 196624 | tf_op jit(solution)/shard_map/psum | solution.py:38
  132.9 0.0 copy-done.6
  132.9 1.6 fusion.4
  134.5 0.0 copy-done
  134.5 2.3 fusion.7
  136.8 0.0 copy-start.4
  136.8 0.0 all-reduce.6.cloned.1.call-update
  136.8 0.0 all-reduce.8.cloned.1.call-start
  136.9 204.0 %all-reduce.6.cloned.1.call-done = f32[384,2048]{1,0:T(8,128)} async-done(((f32[384,2048]{1,0:T(8,128)}), f32[384,2048]{1,0:T(8,128)}) %all-reduce.6.cloned.1.call-update) | async-done | bytes 3145744 | tf_op jit(solution)/shard_map/psum | solution.py:42
  340.9 0.0 copy-done.4
  340.9 2.4 subtract_convert_fusion
  343.3 0.0 copy-start.1
  343.3 1.1 copy-done.1
  344.4 1.3 fusion.8
  345.7 2.7 fusion.3
  348.4 0.0 all-reduce.8.cloned.1.call-update
  348.4 1.5 constant_dynamic-slice_fusion
  349.9 48.9 %all-reduce.8.cloned.1.call-done = f32[384,128]{1,0:T(8,128)} async-done(((f32[384,128]{1,0:T(8,128)}), f32[384,128]{1,0:T(8,128)}) %all-reduce.8.cloned.1.call-update) | async-done | bytes 196624 | tf_op jit(solution)/shard_map/psum | solution.py:53
  398.7 1.0 fusion.5
  399.7 1.3 convolution_convert_fusion
  (8 shorter events, 0.1 us)
Async XLA Ops:
  7.2 127.4 %copy-start = (bf16[128,2048]{1,0:T(8,128)(2,1)S(1)}, bf16[128,2048]{1,0:T(8,128)(2,1)}, u32[]{:S(2)}) copy-start(bf16[128,2048]{1,0:T(8,128)(2,1)} %param.12) | copy-start | bytes 1572868
  10.3 18.0 %copy-start.3 = (s32[384,64]{0,1:T(8,128)S(1)}, s32[384,64]{0,1:T(8,128)}, u32[]{:S(2)}) copy-start(s32[384,64]{0,1:T(8,128)} %param.14) | copy-start | bytes 294916
  10.3 18.0 %copy-start.5 = (s32[384]{0:T(512)S(1)}, s32[384]{0:T(512)}, u32[]{:S(2)}) copy-start(s32[384]{0:T(512)} %param.15) | copy-start | bytes 4612
  10.3 71.6 %all-to-all-start = ((bf16[128,3,2048]{2,1,0:T(4,128)(2,1)}), bf16[128,3,2048]{2,1,0:T(4,128)(2,1)}, u32[]{:S(2)}, u32[]{:S(2)}) async-start(bf16[128,3,2048]{2,1,0:T(4,128)(2,1)} %stack.2), calls=%async_computation | async-start | bytes 4194304 | tf_op jit(solution)/shard_map/all_to_all | solution.py:11
  28.3 104.6 %all-reduce.4.cloned.1.call-start = ((), (), s32[]{:S(2)}) async-start(), calls=%async_computation.1 | async-start | bytes 393216 | tf_op jit(solution)/shard_map/psum | solution.py:38
  28.5 57.3 %copy-start.2 = (bf16[128,2048]{1,0:T(8,128)(2,1)S(1)}, bf16[128,2048]{1,0:T(8,128)(2,1)}, u32[]{:S(2)}) copy-start(bf16[128,2048]{1,0:T(8,128)(2,1)} %param.10) | copy-start | bytes 1572868
  85.9 47.0 %copy-start.6 = (f32[128]{0:T(128)S(1)}, f32[128]{0:T(128)}, u32[]{:S(2)}) copy-start(f32[128]{0:T(128)} %param.11) | copy-start | bytes 1540
  87.2 253.7 %all-reduce.6.cloned.1.call-start = ((), (), s32[]{:S(2)}) async-start(), calls=%async_computation.2 | async-start | bytes 6291456 | tf_op jit(solution)/shard_map/psum | solution.py:42
  136.8 204.1 %copy-start.4 = (f32[2048]{0:T(1024)S(1)}, f32[2048]{0:T(1024)}, u32[]{:S(2)}) copy-start(f32[2048]{0:T(1024)} %param.13) | copy-start | bytes 24580
  136.8 261.9 %all-reduce.8.cloned.1.call-start = ((), (), s32[]{:S(2)}) async-start(), calls=%async_computation.3 | async-start | bytes 393216 | tf_op jit(solution)/shard_map/psum | solution.py:53
  343.3 1.1 copy-start.1
Sparse Core Ops, SparseCore 0:
  87.3 45.5 all-reduce.3
  136.9 203.9 all-reduce.5
  348.5 50.1 all-reduce.7
